TPU v7x, 128 devices: a whole 4x4x4 slice. The times are simulated.
128 devices in a mesh: section: 4 (over z), mp: 32 (over y, x, core).
Axes of the slice: x: 4, y: 4, z: 4, core: 2. Of those that a mesh axis runs over, the one named last changes fastest.
Arguments:
- entering_hidden: bfloat16 [4, 256, 8192], P('section', None, 'mp'), may hold values from -12 to 12
- section_weight: bfloat16 [4, 8192, 8192], P('section', None, 'mp'), may hold values from -0.0625 to 0.0625
- section_norm_gain: bfloat16 [4, 8192], P('section', 'mp'), may hold values from 0.5 to 1.5
- plugin_narrowing_factors: bfloat16 [4, 32, 8192, 64], P('section', 'mp'), may hold values from -0.0625 to 0.0625
- plugin_widening_factors: bfloat16 [4, 32, 64, 8192], P('section', 'mp'), may hold values from -0.75 to 0.75
- reward_head: bfloat16 [8192], P('mp'), may hold values from -0.0625 to 0.0625
- adapter_of_block: int32 [4, 2], replicated, may hold values from 0 to 31
- live_block_rows: int32 [4, 2], P('section'), may hold values from 1 to 128
Outputs:
- hidden_out: bfloat16 [4, 256, 8192], P('section', None, 'mp')
- scores: float32 [4, 256], P('section')
All inputs are finite; a program needn't handle non-finite values.
Results may differ from a plain program's by a relative error of at most 0.022.
Values may be sent and summed in bfloat16 or wider, within the bound.
A program may use at most 64 MiB of HBM per device.

v0:
```python
import jax
import jax.numpy as jnp
from jax import lax
from jax.sharding import PartitionSpec as P

BLOCK = 128


def shifted(value, axis, steps):
    count = lax.axis_size(axis)
    initial, last = (max(0, -steps), min(count, count - steps))
    return lax.ppermute(value, axis, [(source, source + steps) for source in range(initial, last)])


def shards(
    entering_hidden,
    section_weight,
    section_norm_gain,
    plugin_narrowing_factors,
    plugin_widening_factors,
    reward_head,
    adapter_of_block,
    live_block_rows,
):
    sections = lax.axis_size("section")
    section_index = lax.axis_index("section")
    owners = lax.axis_size("mp")
    owner_index = lax.axis_index("mp")
    batches_here, rows, piece_extent = entering_hidden.shape
    micro = batches_here * sections
    width = piece_extent * owners
    blocks = rows // BLOCK
    owned_blocks = plugin_narrowing_factors.shape[1]
    adapters = owned_blocks * owners
    rank_position = plugin_narrowing_factors.shape[3]
    weight = section_weight[0]
    gain = section_norm_gain[0].astype(jnp.float32)
    fed = lax.all_gather(entering_hidden, "section", axis=0, tiled=True)
    up_map_columns = lax.all_to_all(
        plugin_widening_factors, "mp", split_axis=3, concat_axis=1, tiled=True
    )[0]
    up_table = up_map_columns.reshape(adapters, rank_position * piece_extent)

    def layer_of_section(hidden_state, adapter_numbers):
        hidden_f = hidden_state.astype(jnp.float32)
        onehot = (
            adapter_numbers[:, None] == jnp.arange(adapters, dtype=jnp.int32)[None, :]
        ).astype(jnp.bfloat16)
        squares = lax.psum(jnp.sum(hidden_f * hidden_f, axis=1), "mp")
        rescaled_activation = (
            hidden_f * lax.rsqrt(squares / width + 1e-05)[:, None] * gain[None, :]
        ).astype(jnp.bfloat16)
        gathered = lax.all_gather(rescaled_activation, "mp", axis=1, tiled=True)
        base = jnp.dot(gathered, weight, preferred_element_type=jnp.float32)
        local_ids = adapter_numbers - owner_index * owned_blocks
        mine = (local_ids >= 0) & (local_ids < owned_blocks)
        products = []
        for block_number in range(blocks):
            segment = gathered[block_number * BLOCK : (block_number + 1) * BLOCK]
            picked = jnp.clip(local_ids[block_number], 0, owned_blocks - 1)
            products.append(
                lax.cond(
                    mine[block_number],
                    lambda incoming_rows, selected_adapter: jnp.dot(
                        incoming_rows,
                        plugin_narrowing_factors[0, selected_adapter],
                        preferred_element_type=jnp.float32,
                    ),
                    lambda incoming_rows, selected_adapter: jnp.zeros(
                        (BLOCK, rank_position), jnp.float32
                    ),
                    segment,
                    picked,
                )
            )
        compressed_projection = jnp.stack(products)
        compressed_projection = lax.psum(compressed_projection.astype(jnp.bfloat16), "mp")
        chosen_expansion_matrix = (
            jnp.dot(onehot, up_table, preferred_element_type=jnp.float32)
            .astype(jnp.bfloat16)
            .reshape(blocks, rank_position, piece_extent)
        )
        thin_correction = jnp.einsum(
            "sin,sny->siy",
            compressed_projection,
            chosen_expansion_matrix,
            preferred_element_type=jnp.float32,
        ).reshape(rows, piece_extent)
        return (hidden_f + base + 2.0 * thin_correction).astype(jnp.bfloat16)

    def tick(step, carry):
        moving, finished = carry
        arrived = shifted(moving, "section", 1)
        feed_now = lax.dynamic_index_in_dim(fed, jnp.minimum(step, micro - 1), 0, keepdims=False)
        current_signal = jnp.where(section_index == 0, feed_now, arrived)
        selected_adapter = step - section_index
        valid = (selected_adapter >= 0) & (selected_adapter < micro)
        position = jnp.clip(selected_adapter, 0, micro - 1)
        adapter_numbers = lax.dynamic_index_in_dim(adapter_of_block, position, 0, keepdims=False)
        output = layer_of_section(current_signal, adapter_numbers)
        entry_tuple = valid & (section_index == sections - 1)
        previous = lax.dynamic_index_in_dim(finished, position, 0, keepdims=False)
        finished = lax.dynamic_update_index_in_dim(
            finished, jnp.where(entry_tuple, output, previous), position, 0
        )
        return (output, finished)

    start_moving = jnp.zeros((rows, piece_extent), jnp.bfloat16)
    start_finished = jnp.zeros((micro, rows, piece_extent), jnp.bfloat16)
    moving, finished = lax.fori_loop(0, micro + sections - 1, tick, (start_moving, start_finished))
    hidden_out = lax.psum_scatter(
        finished.astype(jnp.float32).astype(jnp.bfloat16),
        "section",
        scatter_dimension=0,
        tiled=True,
    )
    partial_score = jnp.sum(
        hidden_out.astype(jnp.float32) * reward_head.astype(jnp.float32)[None, None, :], axis=2
    )
    raw = lax.psum(partial_score, "mp")
    place = jnp.arange(rows, dtype=jnp.int32) % BLOCK
    limits = jnp.repeat(live_block_rows, BLOCK, axis=1)
    scores = jnp.where(place[None, :] < limits, raw, jnp.float32(0.0))
    return (hidden_out, scores)


def solution(mesh):
    placed = (
        P("section", None, "mp"),
        P("section", None, "mp"),
        P("section", "mp"),
        P("section", "mp", None, None),
        P("section", "mp", None, None),
        P("mp"),
        P(),
        P("section", None),
    )
    return jax.shard_map(
        shards,
        mesh=mesh,
        in_specs=placed,
        out_specs=(P("section", None, "mp"), P("section", None)),
        check_vma=False,
    )
```

profile of v0, /device:TPU:0, one launch (start us, length us, event | category | flops | bytes accessed | tf_op | source)
XLA Modules:
  0.0 1954.4 jit_solution(13879705828689722286)
XLA Ops:
  17.7 45.2 %reduce.1 = bf16[8192,64]{1,0:T(8,128)(2,1)S(1)} reduce(bf16[8192,1,1,64]{3,2,1,0:T(2,128)(2,1)} %bitcast.80, bf16[]{:T(256)} %broadcast.105), dimensions={1,2}, to_apply=%bitcast.49.reduce_sub_computation | reduce | bytes 2097154
  106.2 1752.9 %while.17 = (s32[]{:T(128)}, bf16[256,256]{1,0:T(8,128)(2,1)}, bf16[4,256,256]{2,1,0:T(8,128)(2,1)}, pred[]{:T(512)}, bf16[4,256,256]{2,1,0:T(8,128)(2,1)}, /*in...) while((s32[]{:T(128)}, bf16[256,256]{1,0:T(8,128)(2,1)}, ...), condition=%wide.region_8.9_spmd.clone, body=%wide.region_0.8_spmd.clone.sunk | while | flops 1353712128 | bytes 31792572 | solution.py:110
  114.1 63.3 %psum.36 = f32[256]{0:T(256)S(1)} all-reduce(f32[256]{0:T(256)S(1)} %get-tuple-element.499), channel_id=1, replica_groups=mesh['section'=4,'mp'=32] {'mp'}, use_global_device_ids=true, to_apply=%region_2.2 | all-reduce | flops 256 | bytes 2048 | tf_op jit(solution)/shard_map/while/body/eval_jaxpr/psum | solution.py:49
  181.2 43.1 %all-gather.2.cloned.1.call-done = bf16[256,8192]{1,0:T(8,128)(2,1)} async-done(((bf16[256,256]{1,0:T(8,128)(2,1)}), bf16[256,8192]{1,0:T(8,128)(2,1)}) %all-gather.2.cloned.1.call-update) | async-done | bytes 4194320 | tf_op jit(solution)/shard_map/while/body/eval_jaxpr/all_gather | solution.py:53
  224.3 126.5 %psum.37 = bf16[2,128,64]{1,2,0:T(8,128)(2,1)S(1)} all-reduce(bf16[2,128,64]{1,2,0:T(8,128)(2,1)S(1)} %pad_maximum_fusion.2), channel_id=1, replica_groups=mesh['section'=4,'mp'=32] {'mp'}, use_global_device_ids=true, to_apply=%region_7.7 | all-reduce | flops 16384 | bytes 65536 | tf_op jit(solution)/shard_map/while/body/eval_jaxpr/psum | solution.py:77
  364.4 62.7 %psum.36 = f32[256]{0:T(256)S(1)} all-reduce(f32[256]{0:T(256)S(1)} %get-tuple-element.499), channel_id=1, replica_groups=mesh['section'=4,'mp'=32] {'mp'}, use_global_device_ids=true, to_apply=%region_2.2 | all-reduce | flops 256 | bytes 2048 | tf_op jit(solution)/shard_map/while/body/eval_jaxpr/psum | solution.py:49
  430.9 42.9 %all-gather.2.cloned.1.call-done = bf16[256,8192]{1,0:T(8,128)(2,1)} async-done(((bf16[256,256]{1,0:T(8,128)(2,1)}), bf16[256,8192]{1,0:T(8,128)(2,1)}) %all-gather.2.cloned.1.call-update) | async-done | bytes 4194320 | tf_op jit(solution)/shard_map/while/body/eval_jaxpr/all_gather | solution.py:53
  476.4 123.8 %psum.37 = bf16[2,128,64]{1,2,0:T(8,128)(2,1)S(1)} all-reduce(bf16[2,128,64]{1,2,0:T(8,128)(2,1)S(1)} %pad_maximum_fusion.2), channel_id=1, replica_groups=mesh['section'=4,'mp'=32] {'mp'}, use_global_device_ids=true, to_apply=%region_7.7 | all-reduce | flops 16384 | bytes 65536 | tf_op jit(solution)/shard_map/while/body/eval_jaxpr/psum | solution.py:77
  613.8 62.7 %psum.36 = f32[256]{0:T(256)S(1)} all-reduce(f32[256]{0:T(256)S(1)} %get-tuple-element.499), channel_id=1, replica_groups=mesh['section'=4,'mp'=32] {'mp'}, use_global_device_ids=true, to_apply=%region_2.2 | all-reduce | flops 256 | bytes 2048 | tf_op jit(solution)/shard_map/while/body/eval_jaxpr/psum | solution.py:49
  680.3 42.9 %all-gather.2.cloned.1.call-done = bf16[256,8192]{1,0:T(8,128)(2,1)} async-done(((bf16[256,256]{1,0:T(8,128)(2,1)}), bf16[256,8192]{1,0:T(8,128)(2,1)}) %all-gather.2.cloned.1.call-update) | async-done | bytes 4194320 | tf_op jit(solution)/shard_map/while/body/eval_jaxpr/all_gather | solution.py:53
  723.2 129.1 %psum.37 = bf16[2,128,64]{1,2,0:T(8,128)(2,1)S(1)} all-reduce(bf16[2,128,64]{1,2,0:T(8,128)(2,1)S(1)} %pad_maximum_fusion.2), channel_id=1, replica_groups=mesh['section'=4,'mp'=32] {'mp'}, use_global_device_ids=true, to_apply=%region_7.7 | all-reduce | flops 16384 | bytes 65536 | tf_op jit(solution)/shard_map/while/body/eval_jaxpr/psum | solution.py:77
  863.7 62.7 %psum.36 = f32[256]{0:T(256)S(1)} all-reduce(f32[256]{0:T(256)S(1)} %get-tuple-element.499), channel_id=1, replica_groups=mesh['section'=4,'mp'=32] {'mp'}, use_global_device_ids=true, to_apply=%region_2.2 | all-reduce | flops 256 | bytes 2048 | tf_op jit(solution)/shard_map/while/body/eval_jaxpr/psum | solution.py:49
  930.2 42.4 %all-gather.2.cloned.1.call-done = bf16[256,8192]{1,0:T(8,128)(2,1)} async-done(((bf16[256,256]{1,0:T(8,128)(2,1)}), bf16[256,8192]{1,0:T(8,128)(2,1)}) %all-gather.2.cloned.1.call-update) | async-done | bytes 4194320 | tf_op jit(solution)/shard_map/while/body/eval_jaxpr/all_gather | solution.py:53
  972.6 126.5 %psum.37 = bf16[2,128,64]{1,2,0:T(8,128)(2,1)S(1)} all-reduce(bf16[2,128,64]{1,2,0:T(8,128)(2,1)S(1)} %pad_maximum_fusion.2), channel_id=1, replica_groups=mesh['section'=4,'mp'=32] {'mp'}, use_global_device_ids=true, to_apply=%region_7.7 | all-reduce | flops 16384 | bytes 65536 | tf_op jit(solution)/shard_map/while/body/eval_jaxpr/psum | solution.py:77
  1115.3 62.7 %psum.36 = f32[256]{0:T(256)S(1)} all-reduce(f32[256]{0:T(256)S(1)} %get-tuple-element.499), channel_id=1, replica_groups=mesh['section'=4,'mp'=32] {'mp'}, use_global_device_ids=true, to_apply=%region_2.2 | all-reduce | flops 256 | bytes 2048 | tf_op jit(solution)/shard_map/while/body/eval_jaxpr/psum | solution.py:49
  1181.8 41.3 %all-gather.2.cloned.1.call-done = bf16[256,8192]{1,0:T(8,128)(2,1)} async-done(((bf16[256,256]{1,0:T(8,128)(2,1)}), bf16[256,8192]{1,0:T(8,128)(2,1)}) %all-gather.2.cloned.1.call-update) | async-done | bytes 4194320 | tf_op jit(solution)/shard_map/while/body/eval_jaxpr/all_gather | solution.py:53
  1223.1 126.5 %psum.37 = bf16[2,128,64]{1,2,0:T(8,128)(2,1)S(1)} all-reduce(bf16[2,128,64]{1,2,0:T(8,128)(2,1)S(1)} %pad_maximum_fusion.2), channel_id=1, replica_groups=mesh['section'=4,'mp'=32] {'mp'}, use_global_device_ids=true, to_apply=%region_7.7 | all-reduce | flops 16384 | bytes 65536 | tf_op jit(solution)/shard_map/while/body/eval_jaxpr/psum | solution.py:77
  1363.1 62.7 %psum.36 = f32[256]{0:T(256)S(1)} all-reduce(f32[256]{0:T(256)S(1)} %get-tuple-element.499), channel_id=1, replica_groups=mesh['section'=4,'mp'=32] {'mp'}, use_global_device_ids=true, to_apply=%region_2.2 | all-reduce | flops 256 | bytes 2048 | tf_op jit(solution)/shard_map/while/body/eval_jaxpr/psum | solution.py:49
  1429.6 45.5 %all-gather.2.cloned.1.call-done = bf16[256,8192]{1,0:T(8,128)(2,1)} async-done(((bf16[256,256]{1,0:T(8,128)(2,1)}), bf16[256,8192]{1,0:T(8,128)(2,1)}) %all-gather.2.cloned.1.call-update) | async-done | bytes 4194320 | tf_op jit(solution)/shard_map/while/body/eval_jaxpr/all_gather | solution.py:53
  1475.2 126.5 %psum.37 = bf16[2,128,64]{1,2,0:T(8,128)(2,1)S(1)} all-reduce(bf16[2,128,64]{1,2,0:T(8,128)(2,1)S(1)} %pad_maximum_fusion.2), channel_id=1, replica_groups=mesh['section'=4,'mp'=32] {'mp'}, use_global_device_ids=true, to_apply=%region_7.7 | all-reduce | flops 16384 | bytes 65536 | tf_op jit(solution)/shard_map/while/body/eval_jaxpr/psum | solution.py:77
  1615.2 62.7 %psum.36 = f32[256]{0:T(256)S(1)} all-reduce(f32[256]{0:T(256)S(1)} %get-tuple-element.499), channel_id=1, replica_groups=mesh['section'=4,'mp'=32] {'mp'}, use_global_device_ids=true, to_apply=%region_2.2 | all-reduce | flops 256 | bytes 2048 | tf_op jit(solution)/shard_map/while/body/eval_jaxpr/psum | solution.py:49
  1681.7 45.3 %all-gather.2.cloned.1.call-done = bf16[256,8192]{1,0:T(8,128)(2,1)} async-done(((bf16[256,256]{1,0:T(8,128)(2,1)}), bf16[256,8192]{1,0:T(8,128)(2,1)}) %all-gather.2.cloned.1.call-update) | async-done | bytes 4194320 | tf_op jit(solution)/shard_map/while/body/eval_jaxpr/all_gather | solution.py:53
  1727.0 126.5 %psum.37 = bf16[2,128,64]{1,2,0:T(8,128)(2,1)S(1)} all-reduce(bf16[2,128,64]{1,2,0:T(8,128)(2,1)S(1)} %pad_maximum_fusion.2), channel_id=1, replica_groups=mesh['section'=4,'mp'=32] {'mp'}, use_global_device_ids=true, to_apply=%region_7.7 | all-reduce | flops 16384 | bytes 65536 | tf_op jit(solution)/shard_map/while/body/eval_jaxpr/psum | solution.py:77
  1881.8 64.6 %psum.31 = f32[1,256]{1,0:T(1,128)S(1)} all-reduce(f32[1,256]{1,0:T(1,128)S(1)} %bitcast.87), channel_id=1, replica_groups=mesh['section'=4,'mp'=32] {'mp'}, use_global_device_ids=true, to_apply=%region_11.12 | all-reduce | flops 256 | bytes 2048 | tf_op jit(solution)/shard_map/psum | solution.py:120
  (165 shorter events, 195.2 us)
Async XLA Ops:
  62.9 11.8 copy-start.1
  62.9 11.9 copy-start.2
  62.9 11.9 copy-start
  65.2 24.6 %all-to-all-start = ((bf16[32,2,8192]{2,1,0:T(2,128)(2,1)}), bf16[32,2,8192]{2,1,0:T(2,128)(2,1)S(1)}, u32[]{:S(2)}, u32[]{:S(2)}) async-start(bf16[32,2,8192]{2,1,0:T(2,128)(2,1)} %reshape.80), calls=%async_computation | async-start | bytes 2097152 | tf_op jit(solution)/shard_map/all_to_all | solution.py:39
  106.2 1753.5 %copy-start.3 = (bf16[256]{0:T(256)(128)(2,1)S(1)}, bf16[256]{0:T(256)(128)(2,1)}, u32[]{:S(2)}) copy-start(bf16[256]{0:T(256)(128)(2,1)} %param.19) | copy-start | bytes 1540
  106.2 1840.2 %copy-start.4 = (s32[1,2]{1,0:T(1,128)S(1)}, s32[1,2]{1,0:T(1,128)}, u32[]{:S(2)}) copy-start(s32[1,2]{1,0:T(1,128)} %param.21) | copy-start | bytes 28
  106.2 118.1 %all-gather.2.cloned.1.call-start = ((), (), s32[]{:S(2)}) async-start(), calls=%async_computation.3 | async-start | bytes 4325376 | tf_op jit(solution)/shard_map/while/body/eval_jaxpr/all_gather | solution.py:53
  106.2 6.8 collective-permute-start
  356.4 117.3 %all-gather.2.cloned.1.call-start = ((), (), s32[]{:S(2)}) async-start(), calls=%async_computation.3 | async-start | bytes 4325376 | tf_op jit(solution)/shard_map/while/body/eval_jaxpr/all_gather | solution.py:53
  357.4 6.0 collective-permute-start
  605.9 117.3 %all-gather.2.cloned.1.call-start = ((), (), s32[]{:S(2)}) async-start(), calls=%async_computation.3 | async-start | bytes 4325376 | tf_op jit(solution)/shard_map/while/body/eval_jaxpr/all_gather | solution.py:53
  606.8 6.0 collective-permute-start
  857.9 114.7 %all-gather.2.cloned.1.call-start = ((), (), s32[]{:S(2)}) async-start(), calls=%async_computation.3 | async-start | bytes 4325376 | tf_op jit(solution)/shard_map/while/body/eval_jaxpr/all_gather | solution.py:53
  858.8 3.8 collective-permute-start
  1104.7 118.4 %all-gather.2.cloned.1.call-start = ((), (), s32[]{:S(2)}) async-start(), calls=%async_computation.3 | async-start | bytes 4325376 | tf_op jit(solution)/shard_map/while/body/eval_jaxpr/all_gather | solution.py:53
  1105.7 8.6 collective-permute-start
  1355.2 119.9 %all-gather.2.cloned.1.call-start = ((), (), s32[]{:S(2)}) async-start(), calls=%async_computation.3 | async-start | bytes 4325376 | tf_op jit(solution)/shard_map/while/body/eval_jaxpr/all_gather | solution.py:53
  1356.1 6.0 collective-permute-start
  1607.3 119.7 %all-gather.2.cloned.1.call-start = ((), (), s32[]{:S(2)}) async-start(), calls=%async_computation.3 | async-start | bytes 4325376 | tf_op jit(solution)/shard_map/while/body/eval_jaxpr/all_gather | solution.py:53
  1608.2 6.0 collective-permute-start
  1859.1 21.6 %reduce-scatter.2.cloned.1.call-start = ((), (), s32[]{:S(2)}) async-start(), calls=%async_computation.2 | async-start | bytes 655360 | tf_op jit(solution)/shard_map/reduce_scatter | solution.py:111
Sparse Core Ops, SparseCore 0:
  178.3 45.9 all-gather.1
  428.0 45.7 all-gather.1
  677.4 45.7 all-gather.1
  927.3 45.2 all-gather.1
  1178.9 44.1 all-gather.1
  1426.7 48.3 all-gather.1
  1678.8 48.1 all-gather.1
Sparse Core Ops, SparseCore 1:
  1862.5 18.2 reduce-scatter.1
where the time goes:
time: 1960 us; the launch traced here: 1950 us
  blocking collectives  1400 us (71%)
  waiting for transfers between devices  343 us (18%)
  other arithmetic  65.1 us (3%)
  matrix products  44.3 us (2%)
  local copies, waits for them, and re-layouts  41.1 us (2%)
  starting transfers between devices  32.5 us (2%)
    psum x7, blocking collectives, layer_of_section(): lax.psum(compressed_projection.astype(jnp.bfloat16), 'mp')  885 us
    psum x7, blocking collectives, layer_of_section(): squares = lax.psum(jnp.sum(hidden_f * hidden_f, axis=1), 'mp')  439 us
    all_gather x7, waiting for transfers between devices, layer_of_section(): gathered = lax.all_gather(rescaled_activation, 'mp', axis=1, tiled=True)  303 us
    psum x1, blocking collectives, shards(): raw = lax.psum(partial_score, 'mp')  64.6 us
    unnamed x2, other arithmetic  45.2 us
  transfers between devices with their start and end apart: 16, of which 16 were waited for; matrix products, arithmetic and copies ran while one was open for 1% of the time, Pallas kernels for 0%

commit v1 on v0

--- a/solution.py
+++ b/solution.py
@@ -50,7 +50,10 @@
         rescaled_activation = (
             hidden_f * lax.rsqrt(squares / width + 1e-05)[:, None] * gain[None, :]
         ).astype(jnp.bfloat16)
-        gathered = lax.all_gather(rescaled_activation, "mp", axis=1, tiled=True)
+        gathered = jnp.concatenate(
+            lax.all_to_all(jnp.stack([rescaled_activation] * lax.axis_size("mp")), "mp", 0, 0),
+            axis=1,
+        )
         base = jnp.dot(gathered, weight, preferred_element_type=jnp.float32)
         local_ids = adapter_numbers - owner_index * owned_blocks
         mine = (local_ids >= 0) & (local_ids < owned_blocks)

time: 1960 us -> 2150 us (1.097)
  local copies, waits for them, and re-layouts: 41.1 us -> 114 us
  waiting for transfers between devices: 343 us -> 405 us
  starting transfers between devices: 32.5 us -> 89.1 us
    all_to_all x0 -> x7, waiting for transfers between devices: none -> 356 us  [layer_of_section(): lax.all_to_all(jnp.stack([rescaled_activation] * lax.axis_size('mp')), 'm...]
    all_gather x7 -> x0, waiting for transfers between devices: 303 us -> none  [layer_of_section(): gathered = lax.all_gather(rescaled_activation, 'mp', axis=1, tiled=True)]
    all_to_all x0 -> x7, local copies, waits for them, and re-layouts: none -> 45 us  [layer_of_section(): lax.all_to_all(jnp.stack([rescaled_activation] * lax.axis_size('mp')), 'm...]
    all_to_all x0 -> x7, starting transfers between devices: none -> 33.9 us  [layer_of_section(): lax.all_to_all(jnp.stack([rescaled_activation] * lax.axis_size('mp')), 'm...]
    another operation x0 -> x8, local copies, waits for them, and re-layouts: none -> 24.7 us  [the longest x7 16.8 us: layer_of_section(): jnp.stack([rescaled_activation] * lax.axis_size('mp'))]
    ppermute x7, starting transfers between devices: 25.1 us -> 47.7 us  [shifted(): lax.ppermute(value, axis, [(source, source + steps) for source in range(i...]
  transfers between devices with their start and end apart: 16 -> 16, of which waited for: 16 -> 15; matrix products, arithmetic and copies ran while one was open for 1% -> 1% of each run, Pallas kernels for 0% -> 0%
where the time goes in v1:
time: 2150 us; the launch traced here: 2140 us
  blocking collectives  1410 us (66%)
  waiting for transfers between devices  405 us (19%)
  local copies, waits for them, and re-layouts  114 us (5%)
  starting transfers between devices  89.1 us (4%)
  other arithmetic  60.5 us (3%)
  matrix products  43.1 us (2%)
    psum x7, blocking collectives, layer_of_section(): lax.psum(compressed_projection.astype(jnp.bfloat16), 'mp')  888 us
    psum x7, blocking collectives, layer_of_section(): squares = lax.psum(jnp.sum(hidden_f * hidden_f, axis=1), 'mp')  439 us
    all_to_all x7, waiting for transfers between devices, layer_of_section(): lax.all_to_all(jnp.stack([rescaled_activation] * lax.axis_size('mp')), 'm...  356 us
    psum x1, blocking collectives, shards(): raw = lax.psum(partial_score, 'mp')  64.7 us
    ppermute x7, starting transfers between devices, shifted(): lax.ppermute(value, axis, [(source, source + steps) for source in range(i...  47.7 us
    unnamed x2, other arithmetic  45.2 us
    all_to_all x7, local copies, waits for them, and re-layouts, layer_of_section(): lax.all_to_all(jnp.stack([rescaled_activation] * lax.axis_size('mp')), 'm...  45 us
  transfers between devices with their start and end apart: 16, of which 15 were waited for; matrix products, arithmetic and copies ran while one was open for 1% of the time, Pallas kernels for 0%

profile of v1, /device:TPU:0, one launch (start us, length us, event | category | flops | bytes accessed | tf_op | source)
XLA Modules:
  0.0 2141.4 jit_solution(8399811046746629189)
XLA Ops:
  16.9 45.2 %reduce.1 = bf16[8192,64]{1,0:T(8,128)(2,1)S(1)} reduce(bf16[8192,1,1,64]{3,2,1,0:T(2,128)(2,1)} %bitcast.102, bf16[]{:T(256)} %broadcast.110), dimensions={1,2}, to_apply=%bitcast.56.reduce_sub_computation | reduce | bytes 2097154
  105.3 1932.2 %while.17 = (s32[]{:T(128)}, bf16[256,256]{1,0:T(8,128)(2,1)}, bf16[4,256,256]{2,1,0:T(8,128)(2,1)}, pred[]{:T(512)}, bf16[4,256,256]{2,1,0:T(8,128)(2,1)}, /*in...) while((s32[]{:T(128)}, bf16[256,256]{1,0:T(8,128)(2,1)}, ...), condition=%wide.region_8.9_spmd.clone, body=%wide.region_0.8_spmd.clone.sunk | while | flops 1353712128 | bytes 81862136 | solution.py:113
  113.2 63.4 %psum.36 = f32[256]{0:T(256)S(1)} all-reduce(f32[256]{0:T(256)S(1)} %get-tuple-element.513), channel_id=1, replica_groups=mesh['section'=4,'mp'=32] {'mp'}, use_global_device_ids=true, to_apply=%region_2.2 | all-reduce | flops 256 | bytes 2048 | tf_op jit(solution)/shard_map/while/body/eval_jaxpr/psum | solution.py:49
  187.0 50.9 %all-to-all-done = bf16[32,256,256]{2,1,0:T(8,128)(2,1)} async-done(((bf16[32,256,256]{2,1,0:T(8,128)(2,1)}), bf16[32,256,256]{2,1,0:T(8,128)(2,1)}, u32[]{:S(2)}, u32[]{:S(2)}) %all-to-all-start) | async-done | bytes 4194336 | tf_op jit(solution)/shard_map/while/body/eval_jaxpr/all_to_all | solution.py:54
  244.4 130.2 %psum.37 = bf16[2,128,64]{1,2,0:T(8,128)(2,1)S(1)} all-reduce(bf16[2,128,64]{1,2,0:T(8,128)(2,1)S(1)} %pad_maximum_fusion.2), channel_id=1, replica_groups=mesh['section'=4,'mp'=32] {'mp'}, use_global_device_ids=true, to_apply=%region_7.7 | all-reduce | flops 16384 | bytes 65536 | tf_op jit(solution)/shard_map/while/body/eval_jaxpr/psum | solution.py:80
  388.8 62.7 %psum.36 = f32[256]{0:T(256)S(1)} all-reduce(f32[256]{0:T(256)S(1)} %get-tuple-element.513), channel_id=1, replica_groups=mesh['section'=4,'mp'=32] {'mp'}, use_global_device_ids=true, to_apply=%region_2.2 | all-reduce | flops 256 | bytes 2048 | tf_op jit(solution)/shard_map/while/body/eval_jaxpr/psum | solution.py:49
  462.0 50.9 %all-to-all-done = bf16[32,256,256]{2,1,0:T(8,128)(2,1)} async-done(((bf16[32,256,256]{2,1,0:T(8,128)(2,1)}), bf16[32,256,256]{2,1,0:T(8,128)(2,1)}, u32[]{:S(2)}, u32[]{:S(2)}) %all-to-all-start) | async-done | bytes 4194336 | tf_op jit(solution)/shard_map/while/body/eval_jaxpr/all_to_all | solution.py:54
  531.3 123.8 %psum.37 = bf16[2,128,64]{1,2,0:T(8,128)(2,1)S(1)} all-reduce(bf16[2,128,64]{1,2,0:T(8,128)(2,1)S(1)} %pad_maximum_fusion.2), channel_id=1, replica_groups=mesh['section'=4,'mp'=32] {'mp'}, use_global_device_ids=true, to_apply=%region_7.7 | all-reduce | flops 16384 | bytes 65536 | tf_op jit(solution)/shard_map/while/body/eval_jaxpr/psum | solution.py:80
  666.6 62.7 %psum.36 = f32[256]{0:T(256)S(1)} all-reduce(f32[256]{0:T(256)S(1)} %get-tuple-element.513), channel_id=1, replica_groups=mesh['section'=4,'mp'=32] {'mp'}, use_global_device_ids=true, to_apply=%region_2.2 | all-reduce | flops 256 | bytes 2048 | tf_op jit(solution)/shard_map/while/body/eval_jaxpr/psum | solution.py:49
  739.7 50.9 %all-to-all-done = bf16[32,256,256]{2,1,0:T(8,128)(2,1)} async-done(((bf16[32,256,256]{2,1,0:T(8,128)(2,1)}), bf16[32,256,256]{2,1,0:T(8,128)(2,1)}, u32[]{:S(2)}, u32[]{:S(2)}) %all-to-all-start) | async-done | bytes 4194336 | tf_op jit(solution)/shard_map/while/body/eval_jaxpr/all_to_all | solution.py:54
  797.1 136.3 %psum.37 = bf16[2,128,64]{1,2,0:T(8,128)(2,1)S(1)} all-reduce(bf16[2,128,64]{1,2,0:T(8,128)(2,1)S(1)} %pad_maximum_fusion.2), channel_id=1, replica_groups=mesh['section'=4,'mp'=32] {'mp'}, use_global_device_ids=true, to_apply=%region_7.7 | all-reduce | flops 16384 | bytes 65536 | tf_op jit(solution)/shard_map/while/body/eval_jaxpr/psum | solution.py:80
  947.4 62.7 %psum.36 = f32[256]{0:T(256)S(1)} all-reduce(f32[256]{0:T(256)S(1)} %get-tuple-element.513), channel_id=1, replica_groups=mesh['section'=4,'mp'=32] {'mp'}, use_global_device_ids=true, to_apply=%region_2.2 | all-reduce | flops 256 | bytes 2048 | tf_op jit(solution)/shard_map/while/body/eval_jaxpr/psum | solution.py:49
  1020.5 50.9 %all-to-all-done = bf16[32,256,256]{2,1,0:T(8,128)(2,1)} async-done(((bf16[32,256,256]{2,1,0:T(8,128)(2,1)}), bf16[32,256,256]{2,1,0:T(8,128)(2,1)}, u32[]{:S(2)}, u32[]{:S(2)}) %all-to-all-start) | async-done | bytes 4194336 | tf_op jit(solution)/shard_map/while/body/eval_jaxpr/all_to_all | solution.py:54
  1077.9 124.3 %psum.37 = bf16[2,128,64]{1,2,0:T(8,128)(2,1)S(1)} all-reduce(bf16[2,128,64]{1,2,0:T(8,128)(2,1)S(1)} %pad_maximum_fusion.2), channel_id=1, replica_groups=mesh['section'=4,'mp'=32] {'mp'}, use_global_device_ids=true, to_apply=%region_7.7 | all-reduce | flops 16384 | bytes 65536 | tf_op jit(solution)/shard_map/while/body/eval_jaxpr/psum | solution.py:80
  1228.7 62.7 %psum.36 = f32[256]{0:T(256)S(1)} all-reduce(f32[256]{0:T(256)S(1)} %get-tuple-element.513), channel_id=1, replica_groups=mesh['section'=4,'mp'=32] {'mp'}, use_global_device_ids=true, to_apply=%region_2.2 | all-reduce | flops 256 | bytes 2048 | tf_op jit(solution)/shard_map/while/body/eval_jaxpr/psum | solution.py:49
  1301.9 50.9 %all-to-all-done = bf16[32,256,256]{2,1,0:T(8,128)(2,1)} async-done(((bf16[32,256,256]{2,1,0:T(8,128)(2,1)}), bf16[32,256,256]{2,1,0:T(8,128)(2,1)}, u32[]{:S(2)}, u32[]{:S(2)}) %all-to-all-start) | async-done | bytes 4194336 | tf_op jit(solution)/shard_map/while/body/eval_jaxpr/all_to_all | solution.py:54
  1359.2 124.3 %psum.37 = bf16[2,128,64]{1,2,0:T(8,128)(2,1)S(1)} all-reduce(bf16[2,128,64]{1,2,0:T(8,128)(2,1)S(1)} %pad_maximum_fusion.2), channel_id=1, replica_groups=mesh['section'=4,'mp'=32] {'mp'}, use_global_device_ids=true, to_apply=%region_7.7 | all-reduce | flops 16384 | bytes 65536 | tf_op jit(solution)/shard_map/while/body/eval_jaxpr/psum | solution.py:80
  1498.1 62.7 %psum.36 = f32[256]{0:T(256)S(1)} all-reduce(f32[256]{0:T(256)S(1)} %get-tuple-element.513), channel_id=1, replica_groups=mesh['section'=4,'mp'=32] {'mp'}, use_global_device_ids=true, to_apply=%region_2.2 | all-reduce | flops 256 | bytes 2048 | tf_op jit(solution)/shard_map/while/body/eval_jaxpr/psum | solution.py:49
  1571.2 50.9 %all-to-all-done = bf16[32,256,256]{2,1,0:T(8,128)(2,1)} async-done(((bf16[32,256,256]{2,1,0:T(8,128)(2,1)}), bf16[32,256,256]{2,1,0:T(8,128)(2,1)}, u32[]{:S(2)}, u32[]{:S(2)}) %all-to-all-start) | async-done | bytes 4194336 | tf_op jit(solution)/shard_map/while/body/eval_jaxpr/all_to_all | solution.py:54
  1628.5 124.3 %psum.37 = bf16[2,128,64]{1,2,0:T(8,128)(2,1)S(1)} all-reduce(bf16[2,128,64]{1,2,0:T(8,128)(2,1)S(1)} %pad_maximum_fusion.2), channel_id=1, replica_groups=mesh['section'=4,'mp'=32] {'mp'}, use_global_device_ids=true, to_apply=%region_7.7 | all-reduce | flops 16384 | bytes 65536 | tf_op jit(solution)/shard_map/while/body/eval_jaxpr/psum | solution.py:80
  1777.0 62.7 %psum.36 = f32[256]{0:T(256)S(1)} all-reduce(f32[256]{0:T(256)S(1)} %get-tuple-element.513), channel_id=1, replica_groups=mesh['section'=4,'mp'=32] {'mp'}, use_global_device_ids=true, to_apply=%region_2.2 | all-reduce | flops 256 | bytes 2048 | tf_op jit(solution)/shard_map/while/body/eval_jaxpr/psum | solution.py:49
  1850.1 50.9 %all-to-all-done = bf16[32,256,256]{2,1,0:T(8,128)(2,1)} async-done(((bf16[32,256,256]{2,1,0:T(8,128)(2,1)}), bf16[32,256,256]{2,1,0:T(8,128)(2,1)}, u32[]{:S(2)}, u32[]{:S(2)}) %all-to-all-start) | async-done | bytes 4194336 | tf_op jit(solution)/shard_map/while/body/eval_jaxpr/all_to_all | solution.py:54
  1907.4 124.3 %psum.37 = bf16[2,128,64]{1,2,0:T(8,128)(2,1)S(1)} all-reduce(bf16[2,128,64]{1,2,0:T(8,128)(2,1)S(1)} %pad_maximum_fusion.2), channel_id=1, replica_groups=mesh['section'=4,'mp'=32] {'mp'}, use_global_device_ids=true, to_apply=%region_7.7 | all-reduce | flops 16384 | bytes 65536 | tf_op jit(solution)/shard_map/while/body/eval_jaxpr/psum | solution.py:80
  2069.3 64.7 %psum.31 = f32[1,256]{1,0:T(1,128)S(1)} all-reduce(f32[1,256]{1,0:T(1,128)S(1)} %bitcast.108), channel_id=1, replica_groups=mesh['section'=4,'mp'=32] {'mp'}, use_global_device_ids=true, to_apply=%region_11.12 | all-reduce | flops 256 | bytes 2048 | tf_op jit(solution)/shard_map/psum | solution.py:123
  (176 shorter events, 337.0 us)
Async XLA Ops:
  64.3 24.6 %all-to-all-start.1 = ((bf16[32,2,8192]{2,1,0:T(2,128)(2,1)}), bf16[32,2,8192]{2,1,0:T(2,128)(2,1)S(1)}, u32[]{:S(2)}, u32[]{:S(2)}) async-start(bf16[32,2,8192]{2,1,0:T(2,128)(2,1)} %reshape.110), calls=%async_computation.1 | async-start | bytes 2097152 | tf_op jit(solution)/shard_map/all_to_all | solution.py:39
  71.8 2.1 copy-start.1
  71.8 2.2 copy-start.2
  71.8 2.2 copy-start
  71.8 1996.4 %reduce-scatter.2.cloned.1.call-start = ((), (), s32[]{:S(2)}) async-start(), calls=%async_computation.3 | async-start | bytes 655360 | tf_op jit(solution)/shard_map/reduce_scatter | solution.py:114
  105.3 1932.2 %copy-start.3 = (bf16[256]{0:T(256)(128)(2,1)S(1)}, bf16[256]{0:T(256)(128)(2,1)}, u32[]{:S(2)}) copy-start(bf16[256]{0:T(256)(128)(2,1)} %param.19) | copy-start | bytes 1540
  105.3 2028.7 %copy-start.4 = (s32[1,2]{1,0:T(1,128)S(1)}, s32[1,2]{1,0:T(1,128)}, u32[]{:S(2)}) copy-start(s32[1,2]{1,0:T(1,128)} %param.21) | copy-start | bytes 28
  105.3 6.8 collective-permute-start
  179.1 58.8 %all-to-all-start = ((bf16[32,256,256]{2,1,0:T(8,128)(2,1)}), bf16[32,256,256]{2,1,0:T(8,128)(2,1)}, u32[]{:S(2)}, u32[]{:S(2)}) async-start(bf16[32,256,256]{2,1,0:T(8,128)(2,1)} %stack.75), calls=%async_computation | async-start | bytes 8388608 | tf_op jit(solution)/shard_map/while/body/eval_jaxpr/all_to_all | solution.py:54
  381.2 6.6 collective-permute-start
  454.0 58.8 %all-to-all-start = ((bf16[32,256,256]{2,1,0:T(8,128)(2,1)}), bf16[32,256,256]{2,1,0:T(8,128)(2,1)}, u32[]{:S(2)}, u32[]{:S(2)}) async-start(bf16[32,256,256]{2,1,0:T(8,128)(2,1)} %stack.75), calls=%async_computation | async-start | bytes 8388608 | tf_op jit(solution)/shard_map/while/body/eval_jaxpr/all_to_all | solution.py:54
  527.2 1.6 slice-start
  661.7 3.8 collective-permute-start
  731.8 58.8 %all-to-all-start = ((bf16[32,256,256]{2,1,0:T(8,128)(2,1)}), bf16[32,256,256]{2,1,0:T(8,128)(2,1)}, u32[]{:S(2)}, u32[]{:S(2)}) async-start(bf16[32,256,256]{2,1,0:T(8,128)(2,1)} %stack.75), calls=%async_computation | async-start | bytes 8388608 | tf_op jit(solution)/shard_map/while/body/eval_jaxpr/all_to_all | solution.py:54
  940.0 6.3 collective-permute-start
  1012.6 58.8 %all-to-all-start = ((bf16[32,256,256]{2,1,0:T(8,128)(2,1)}), bf16[32,256,256]{2,1,0:T(8,128)(2,1)}, u32[]{:S(2)}, u32[]{:S(2)}) async-start(bf16[32,256,256]{2,1,0:T(8,128)(2,1)} %stack.75), calls=%async_computation | async-start | bytes 8388608 | tf_op jit(solution)/shard_map/while/body/eval_jaxpr/all_to_all | solution.py:54
  1208.8 18.9 collective-permute-start
  1293.9 58.8 %all-to-all-start = ((bf16[32,256,256]{2,1,0:T(8,128)(2,1)}), bf16[32,256,256]{2,1,0:T(8,128)(2,1)}, u32[]{:S(2)}, u32[]{:S(2)}) async-start(bf16[32,256,256]{2,1,0:T(8,128)(2,1)} %stack.75), calls=%async_computation | async-start | bytes 8388608 | tf_op jit(solution)/shard_map/while/body/eval_jaxpr/all_to_all | solution.py:54
  1490.2 6.9 collective-permute-start
  1563.3 58.8 %all-to-all-start = ((bf16[32,256,256]{2,1,0:T(8,128)(2,1)}), bf16[32,256,256]{2,1,0:T(8,128)(2,1)}, u32[]{:S(2)}, u32[]{:S(2)}) async-start(bf16[32,256,256]{2,1,0:T(8,128)(2,1)} %stack.75), calls=%async_computation | async-start | bytes 8388608 | tf_op jit(solution)/shard_map/while/body/eval_jaxpr/all_to_all | solution.py:54
  1759.5 16.4 collective-permute-start
  1842.2 58.8 %all-to-all-start = ((bf16[32,256,256]{2,1,0:T(8,128)(2,1)}), bf16[32,256,256]{2,1,0:T(8,128)(2,1)}, u32[]{:S(2)}, u32[]{:S(2)}) async-start(bf16[32,256,256]{2,1,0:T(8,128)(2,1)} %stack.75), calls=%async_computation | async-start | bytes 8388608 | tf_op jit(solution)/shard_map/while/body/eval_jaxpr/all_to_all | solution.py:54
Sparse Core Ops, SparseCore 0:
  2037.6 30.5 reduce-scatter.1
